TPU v7x, 128 devices: a whole 4x4x4 slice. The times are simulated.
128 devices in a mesh: ctx: 16 (over z, y), head: 8 (over x, core).
Axes of the slice: x: 4, y: 4, z: 4, core: 2. Of those that a mesh axis runs over, the one named last changes fastest.
Arguments:
- queries: bfloat16 [16384, 12288], P('ctx', 'head'), may hold values from -24 to 24
- key_rows: bfloat16 [16384, 768], P('ctx'), may hold values from -6 to 6
- value_rows: bfloat16 [16384, 512], P('ctx'), may hold values from -6 to 6
- comp_key_weight: float32 [32, 768], replicated, may hold values from 0.35355338 to 0.70710677
- comp_value_weight: float32 [32, 512], replicated, may hold values from 0.17677669 to 0.53033006
- block_picks: int32 [64, 4, 16], P('ctx'), may hold values from 0 to 252, as said below
- gate_logits: float32 [16384, 3, 64], P('ctx', None, 'head'), may hold values from -6 to 6
- out_weight: bfloat16 [8192, 2560], P('head'), may hold values from -0.25 to 0.25
Outputs:
- layer_out: bfloat16 [16384, 2560], P(('ctx', 'head'))
Inputs may be any that keep to these rules, and one draw needn't show every extreme that they name: `block_picks`: for each group, the lists of the 256-position query blocks held by one ctx shard name exactly 1024 / 256 distinct blocks of each earlier shard and of their own shard, and none of later shards; the own-shard blocks named are the first blocks of those query blocks. Every list names the first block of its own query block. Names may repeat within a list.
All inputs are finite; a program needn't handle non-finite values.
Results may differ from a plain program's by a relative error of at most 0.03.
Values may be sent and summed in bfloat16 or wider, within the bound.
A program may use at most 128 MiB of HBM per device.

v0:
```python
import jax
import jax.numpy as jnp
from jax import lax
from jax.sharding import PartitionSpec as P

HEADS = 64
GROUPS = 4
QUERY_KEY_WIDTH = 192
DV = 128
CBLK = 32
KBLK = 64
PICKS = 16
WINDOW = 512
QBLK = 256
NEG_FILL = -1e30


def shifted(block, axis, distance):
    devices = range(lax.axis_size(axis))
    route = [(i - distance, i) for i in devices if i - distance in devices]
    return lax.ppermute(block, axis, route)


def softmax_parts(scores, keep_mask):
    row_top = jnp.max(jnp.where(keep_mask, scores, NEG_FILL), axis=-1, keepdims=True)
    weights = jnp.where(keep_mask, jnp.exp(scores - row_top), 0.0)
    return (weights.astype(jnp.bfloat16), jnp.sum(weights, axis=-1))


def local(
    queries,
    key_rows,
    value_rows,
    comp_key_weight,
    comp_value_weight,
    block_picks,
    gate_logits,
    out_weight,
):
    tok_rows = queries.shape[0]
    heads_here = queries.shape[1] // QUERY_KEY_WIDTH
    shard_index = lax.axis_index("ctx")
    group_index = lax.axis_index("head") * heads_here // (HEADS // GROUPS)
    lane_count = QUERY_KEY_WIDTH + DV
    per_owner = tok_rows // KBLK
    query_blocks = tok_rows // QBLK
    score_scale = QUERY_KEY_WIDTH ** (-0.5)
    own_keys = lax.dynamic_slice_in_dim(key_rows, group_index * QUERY_KEY_WIDTH, QUERY_KEY_WIDTH, 1)
    own_values = lax.dynamic_slice_in_dim(value_rows, group_index * DV, DV, 1)
    packed = jnp.concatenate([own_keys, own_values], axis=1).reshape(per_owner, KBLK * lane_count)
    query_heads = queries.reshape(tok_rows, heads_here, QUERY_KEY_WIDTH)
    block_queries = queries.reshape(query_blocks, QBLK, heads_here, QUERY_KEY_WIDTH)
    positions = shard_index * tok_rows + jnp.arange(tok_rows, dtype=jnp.int32)
    query_pos = positions.reshape(query_blocks, QBLK)
    gates = jax.nn.sigmoid(gate_logits)
    key_weight = lax.dynamic_slice_in_dim(
        comp_key_weight, group_index * QUERY_KEY_WIDTH, QUERY_KEY_WIDTH, 1
    )
    value_weight = lax.dynamic_slice_in_dim(comp_value_weight, group_index * DV, DV, 1)
    comp_keys = jnp.sum(
        own_keys.reshape(tok_rows // CBLK, CBLK, QUERY_KEY_WIDTH).astype(jnp.float32)
        * key_weight[None],
        axis=1,
    ).astype(jnp.bfloat16)
    comp_values = jnp.sum(
        own_values.reshape(tok_rows // CBLK, CBLK, DV).astype(jnp.float32) * value_weight[None],
        axis=1,
    ).astype(jnp.bfloat16)
    all_comp_keys, all_comp_values = (
        lax.all_gather(comp_keys, "ctx", axis=0, tiled=True),
        lax.all_gather(comp_values, "ctx", axis=0, tiled=True),
    )
    comp_count = all_comp_keys.shape[0]
    comp_ends = (jnp.arange(comp_count, dtype=jnp.int32) + 1) * CBLK - 1
    row_span = min(512, tok_rows)

    def comp_span(span_index):
        first_row = span_index * row_span
        span_queries = lax.dynamic_slice_in_dim(query_heads, first_row, row_span, 0)
        span_pos = lax.dynamic_slice_in_dim(positions, first_row, row_span, 0)
        scores = (
            jnp.einsum(
                "thc,nc->thn", span_queries, all_comp_keys, preferred_element_type=jnp.float32
            )
            * score_scale
        )
        keep_mask = comp_ends[None, None, :] <= span_pos[:, None, None]
        weights, weight_sum = softmax_parts(scores, keep_mask)
        span_out = jnp.einsum(
            "thn,nd->thd", weights, all_comp_values, preferred_element_type=jnp.float32
        )
        return span_out / jnp.maximum(weight_sum, 1.0)[..., None]

    comp_out = lax.map(comp_span, jnp.arange(tok_rows // row_span, dtype=jnp.int32)).reshape(
        tok_rows, heads_here, DV
    )
    rim_rows = shifted(packed[per_owner - WINDOW // KBLK :], "ctx", 1)
    extended = jnp.concatenate([rim_rows, packed], axis=0).reshape(WINDOW + tok_rows, lane_count)
    window_spans = jnp.stack(
        [
            extended[span_index * QBLK : span_index * QBLK + WINDOW + QBLK]
            for span_index in range(query_blocks)
        ]
    )
    win_scores = (
        jnp.einsum(
            "bqhc,bkc->bqhk",
            block_queries,
            window_spans[..., :QUERY_KEY_WIDTH],
            preferred_element_type=jnp.float32,
        )
        * score_scale
    )
    key_pos = (
        shard_index * tok_rows
        - WINDOW
        + jnp.arange(query_blocks, dtype=jnp.int32)[:, None] * QBLK
        + jnp.arange(WINDOW + QBLK, dtype=jnp.int32)[None, :]
    )
    keep_mask = (
        (key_pos[:, None, :] >= 0)
        & (key_pos[:, None, :] <= query_pos[:, :, None])
        & (key_pos[:, None, :] >= query_pos[:, :, None] - WINDOW)
    )
    win_weights, win_sum = softmax_parts(win_scores, keep_mask[:, :, None, :])
    win_out = (
        jnp.einsum(
            "uzai,uix->uzax",
            win_weights,
            window_spans[..., QUERY_KEY_WIDTH:],
            preferred_element_type=jnp.float32,
        )
        / win_sum[..., None]
    )
    my_picks = lax.dynamic_index_in_dim(block_picks, group_index, 1, keepdims=False)
    flat_picks = my_picks.reshape(query_blocks * PICKS)
    gathered = lax.all_gather(packed, "ctx", axis=0, tiled=True)
    tiled_row_groups = gathered[flat_picks]
    tiled_row_groups = tiled_row_groups.reshape(query_blocks, PICKS * KBLK, lane_count)
    pick_order = jnp.arange(PICKS, dtype=jnp.int32)
    repeated = jnp.any(
        (my_picks[:, :, None] == my_picks[:, None, :])
        & (pick_order[None, None, :] < pick_order[None, :, None]),
        axis=-1,
    )
    pick_pos = (my_picks[:, :, None] * KBLK + jnp.arange(KBLK, dtype=jnp.int32)).reshape(
        query_blocks, PICKS * KBLK
    )
    live_mask = jnp.repeat(jnp.logical_not(repeated), KBLK, axis=1)
    keep_mask = (pick_pos[:, None, :] <= query_pos[:, :, None]) & live_mask[:, None, :]
    sel_scores = (
        jnp.einsum(
            "bqhc,bkc->bqhk",
            block_queries,
            tiled_row_groups[..., :QUERY_KEY_WIDTH],
            preferred_element_type=jnp.float32,
        )
        * score_scale
    )
    selected_weights, selected_sum = softmax_parts(sel_scores, keep_mask[:, :, None, :])
    sel_out = (
        jnp.einsum(
            "uzai,uix->uzax",
            selected_weights,
            tiled_row_groups[..., QUERY_KEY_WIDTH:],
            preferred_element_type=jnp.float32,
        )
        / selected_sum[..., None]
    )
    mixed = (
        gates[:, 0, :, None] * comp_out
        + gates[:, 1, :, None] * sel_out.reshape(tok_rows, heads_here, DV)
        + gates[:, 2, :, None] * win_out.reshape(tok_rows, heads_here, DV)
    )
    attended = mixed.astype(jnp.bfloat16).reshape(tok_rows, heads_here * DV)
    return lax.psum_scatter(
        jnp.dot(attended, out_weight, preferred_element_type=jnp.float32).astype(jnp.bfloat16),
        "head",
        scatter_dimension=0,
        tiled=True,
    )


def solution(mesh):
    placed = (
        P("ctx", "head"),
        P("ctx", None),
        P("ctx", None),
        P(),
        P(),
        P("ctx", None, None),
        P("ctx", None, "head"),
        P("head", None),
    )
    return jax.shard_map(
        local, mesh=mesh, in_specs=placed, out_specs=P(("ctx", "head"), None), check_vma=False
    )
```

profile of v0, /device:TPU:0, one launch (start us, length us, event | category | flops | bytes accessed | tf_op | source)
XLA Modules:
  0.0 297.9 jit_solution(15637494506940244456)
XLA Ops:
  9.9 1.7 reshape.226
  13.0 4.3 %collective-permute-start = (bf16[8,20480]{1,0:T(8,128)(2,1)}, bf16[8,20480]{1,0:T(8,128)(2,1)}, u32[]{:S(2)}, u32[]{:S(2)}) collective-permute-start(bf16[8,20480]{1,0:T(8,128)(2,1)} %slice.53), channel_id=1, source_target_pairs={{0,8},{8,16},{16,24},{24,32},{32,40},{40,48},{48,56},{56,64},{64,7... | collective-permute-start | bytes 983048 | tf_op jit(solution)/shard_map/ppermute | solution.py:21
  26.5 3.2 %copy.73 = bf16[1024,1536]{0,1:T(8,128)(2,1)S(1)} copy(bf16[1024,1536]{1,0:T(8,128)(2,1)} %param.10) | data formatting | bytes 6291456 | tf_op args[0]
  32.0 26.6 %all_gather.9 = bf16[512,192]{1,0:T(8,128)(2,1)} all-gather(bf16[32,192]{1,0:T(8,128)(2,1)S(1)} %multiply_reduce_fusion), channel_id=1, replica_groups=mesh['ctx'=16,'head'=8] {'ctx'}, dimensions={0}, use_global_device_ids=true | all-gather | bytes 208896 | tf_op jit(solution)/shard_map/all_gather | solution.py:70
  61.5 22.6 %all_gather.10 = bf16[512,128]{1,0:T(8,128)(2,1)S(1)} all-gather(bf16[32,128]{1,0:T(8,128)(2,1)S(1)} %multiply_reduce_fusion.1), channel_id=1, replica_groups=mesh['ctx'=16,'head'=8] {'ctx'}, dimensions={0}, use_global_device_ids=true | all-gather | bytes 139264 | tf_op jit(solution)/shard_map/all_gather | solution.py:71
  86.2 3.0 compare_and_fusion.1
  89.6 30.3 %while.11 = (s32[]{:T(128)}, f32[2,512,8,128]{3,2,1,0:T(8,128)}, s32[2]{0:T(128)}, s32[1024]{0:T(1024)}, bf16[1024,8,192]{0,2,1:T(8,128)(2,1)S(1)}, /*index=5*/b...) while((s32[]{:T(128)}, f32[2,512,8,128]{3,2,1,0:T(8,128)}, ...), condition=%wide.region_5.6_spmd.clone, body=%wide.region_2.5_spmd.clone.sunk | while | flops 1357649920 | bytes 33974984 | solution.py:94
  93.2 5.5 %fusion.113 = (f32[512,8]{0,1:T(8,128)S(1)}, bf16[512,8,512]{0,2,1:T(8,128)(2,1)}) fusion(f32[512,8,512]{0,2,1:T(8,128)S(1)} %fusion.112, pred[512,512]{0,1:T(8,128)(4,1)S(1)} %broadcast_compare_fusion.3), kind=kOutput, calls=%fused_computation.122.clone.1 | output fusion | flops 14680575 | bytes 12861440 | tf_op jit(solution)/shard_map/while/body/eval_jaxpr/sub | solution.py:26
  98.8 3.4 %divide_bitcast_fusion.2 = f32[1,512,8,128]{3,1,2,0:T(8,128)S(1)} fusion(bf16[512,8,512]{0,2,1:T(8,128)(2,1)} %get-tuple-element.158, f32[512,8]{0,1:T(8,128)S(1)} %broadcast_maximum_fusion.2, bf16[512,128]{1,0:T(8,128)(2,1)S(1)} %get-tuple-element.188), kind=kOutput, calls=%fused_computation.13.clone.1 | convolution fusion | flops 537395200 | bytes 6438912 | tf_op jit(solution)/shard_map/while/body/eval_jaxpr/thn,nd->thd/dot_general | solution.py:89
  102.2 2.6 copy_dynamic-update-slice_fusion.2
  106.6 1.5 fusion.112
  108.4 5.5 %fusion.113 = (f32[512,8]{0,1:T(8,128)S(1)}, bf16[512,8,512]{0,2,1:T(8,128)(2,1)}) fusion(f32[512,8,512]{0,2,1:T(8,128)S(1)} %fusion.112, pred[512,512]{0,1:T(8,128)(4,1)S(1)} %broadcast_compare_fusion.3), kind=kOutput, calls=%fused_computation.122.clone.1 | output fusion | flops 14680575 | bytes 12861440 | tf_op jit(solution)/shard_map/while/body/eval_jaxpr/sub | solution.py:26
  113.9 3.4 %divide_bitcast_fusion.2 = f32[1,512,8,128]{3,1,2,0:T(8,128)S(1)} fusion(bf16[512,8,512]{0,2,1:T(8,128)(2,1)} %get-tuple-element.158, f32[512,8]{0,1:T(8,128)S(1)} %broadcast_maximum_fusion.2, bf16[512,128]{1,0:T(8,128)(2,1)S(1)} %get-tuple-element.188), kind=kOutput, calls=%fused_computation.13.clone.1 | convolution fusion | flops 537395200 | bytes 6438912 | tf_op jit(solution)/shard_map/while/body/eval_jaxpr/thn,nd->thd/dot_general | solution.py:89
  117.4 2.6 copy_dynamic-update-slice_fusion.2
  120.6 3.9 %reshape.229 = bf16[4,256,8,192]{1,0,3,2:T(4,128)(2,1)} reshape(bf16[1024,1536]{0,1:T(8,128)(2,1)S(1)} %bitcast.144) | data formatting | bytes 6291456 | tf_op jit(solution)/shard_map/reshape | solution.py:52
  127.8 3.3 %compare_and_fusion = pred[4,256,1024]{1,2,0:T(8,128)(4,1)} fusion(s32[4,256]{1,0:T(4,128)S(1)} %copy-done.8, s32[4,1024]{1,0:T(4,128)S(1)} %broadcast_add_fusion, pred[4,1024]{1,0:T(4,128)(4,1)S(1)} %and.51), kind=kLoop, calls=%fused_computation.55 | loop fusion | flops 2097152 | bytes 1073152 | tf_op jit(solution)/shard_map/and | solution.py:150
  134.5 2.8 stack.15
  137.3 2.1 copy.89
  139.3 2.6 stack.16
  142.0 2.1 copy.90
  144.0 3.0 pad_maximum_fusion
  147.0 15.6 %fusion.88 = (f32[4,256,8]{1,2,0:T(8,128)S(1)}, bf16[4,256,8,768]{1,3,2,0:T(8,128)(2,1)}) fusion(pred[4,256,768]{1,2,0:T(8,128)(4,1)} %compare_and_fusion.1, bf16[4,256,8,192]{1,0,3,2:T(4,128)(2,1)S(1)} %copy-done.2, bf16[4,768,320]{1,2,0:T(8,128)(2,1)} %pad_maximum_fusion), kind=kOutput, calls=%fused_computation.124 | convolution fusion | flops 4875878912 | bytes 22839296 | tf_op jit(solution)/shard_map/sub | solution.py:26
  162.6 7.8 %broadcast_divide_fusion = f32[4,256,8,128]{3,1,2,0:T(8,128)S(1)} fusion(f32[4,256,8]{1,2,0:T(8,128)S(1)} %get-tuple-element.103, bf16[4,256,8,768]{1,3,2,0:T(8,128)(2,1)} %get-tuple-element.104, bf16[1,768,320]{1,2,0:T(8,128)(2,1)} %get-tuple-element.99, bf16[1,768,320]{1,2,0:T(8,128)(2,1)} %get-tuple-element.98, bf16[1,768,320]{1,2,0:T(8,128)(2,1)} %copy.90, ...), kind=kOutput, calls=%fused_computation.61 | convolution fusion | flops 1614807040 | bytes 18776064 | tf_op jit(solution)/shard_map/uzai,uix->uzax/dot_general | solution.py:127
  170.4 4.5 %copy.94 = f32[4,256,8,128]{3,2,1,0:T(8,128)} copy(f32[4,256,8,128]{3,1,2,0:T(8,128)S(1)} %broadcast_divide_fusion) | data formatting | bytes 8388608 | tf_op jit(solution)/shard_map/div | solution.py:127
  174.9 9.8 %gather_fusion = bf16[64,20480]{1,0:T(8,128)(2,1)S(1)} fusion(bf16[256,20480]{1,0:T(8,128)(2,1)} %all-gather.2.cloned.1.call-done, s32[1024]{0:T(1024)S(1)} %pad_clamp_fusion), kind=kCustom, calls=%fused_computation | custom fusion | bytes 5243136 | tf_op jit(solution)/shard_map/gather | solution.py:138
  184.7 4.7 %reshape.228 = bf16[4,1024,320]{2,1,0:T(8,128)(2,1)} reshape(bf16[64,20480]{1,0:T(8,128)(2,1)S(1)} %gather_fusion) | data formatting | bytes 5242880 | tf_op jit(solution)/shard_map/reshape | solution.py:139
  189.4 20.7 %fusion.93 = (f32[4,256,8]{1,2,0:T(8,128)S(1)}, bf16[4,256,8,1024]{1,3,2,0:T(8,128)(2,1)}) fusion(pred[4,256,1024]{1,2,0:T(8,128)(4,1)} %compare_and_fusion, bf16[4,256,8,192]{1,0,3,2:T(4,128)(2,1)} %reshape.229, bf16[4,1024,320]{2,1,0:T(8,128)(2,1)} %reshape.228), kind=kOutput, calls=%fused_computation.125 | convolution fusion | flops 6501172224 | bytes 29392896 | tf_op jit(solution)/shard_map/sub | solution.py:26
  210.2 11.4 %fusion.46 = f32[4,256,8,128]{3,1,2,0:T(8,128)S(1)} fusion(bf16[4,256,8,1024]{1,3,2,0:T(8,128)(2,1)} %get-tuple-element.106, f32[4,256,8]{1,2,0:T(8,128)S(1)} %get-tuple-element.105, bf16[4,1024,320]{2,1,0:T(8,128)(2,1)} %reshape.228), kind=kOutput, calls=%fused_computation.58 | convolution fusion | flops 2148532224 | bytes 22052864 | tf_op jit(solution)/shard_map/uzai,uix->uzax/dot_general | solution.py:162
  221.6 4.4 %copy.86 = f32[4,256,8,128]{3,2,1,0:T(8,128)} copy(f32[4,256,8,128]{3,1,2,0:T(8,128)S(1)} %fusion.46) | data formatting | bytes 8388608 | tf_op jit(solution)/shard_map/div | solution.py:162
  228.3 3.0 %mul.146 = f32[1024,8,128]{2,1,0:T(8,128)} broadcast(f32[1024,8]{1,0:T(8,128)S(1)} %copy-done.5), dimensions={0,1} | broadcast | bytes 4227072 | tf_op jit(solution)/shard_map/mul | solution.py:173
  231.3 19.5 %convolution_convert_fusion = bf16[1024,2560]{1,0:T(8,128)(2,1)} fusion(bf16[1024,2560]{1,0:T(8,128)(2,1)} %param.17, f32[128,8,8,128]{3,2,1,0:T(8,128)} %bitcast.148, f32[128,8,8,128]{3,2,1,0:T(8,128)} %bitcast.147, f32[128,8,8,128]{3,2,1,0:T(8,128)} %bitcast.149, f32[128,8,8,128]{3,2,1,0:T(8,128)S(1)} %bitcast.146, f32[128,8,8,128]{3,2,1,0:T(8,128)} %bitcast.32, ...), kind=kOutput, calls=%fused_computation.48 | convolution fusion | flops 5377622016 | bytes 35651584 | tf_op jit(solution)/shard_map/dot_general | solution.py:177
  250.8 39.7 %reduce-scatter.2.cloned.1.call-done = bf16[128,2560]{1,0:T(8,128)(2,1)} async-done(((bf16[1024,2560]{1,0:T(8,128)(2,1)}), bf16[128,2560]{1,0:T(8,128)(2,1)}) %reduce-scatter.2.cloned.1.call-update) | async-done | bytes 655376 | tf_op jit(solution)/shard_map/reduce_scatter | solution.py:176
  (90 shorter events, 35.7 us)
Async XLA Ops:
  6.5 1.4 copy-start
  6.5 168.4 %all-gather.2.cloned.1.call-start = ((), (), s32[]{:S(2)}) async-start(), calls=%async_computation.1 | async-start | bytes 11141120 | tf_op jit(solution)/shard_map/all_gather | solution.py:137
  11.6 278.9 %reduce-scatter.2.cloned.1.call-start = ((), (), s32[]{:S(2)}) async-start(), calls=%async_computation.2 | async-start | bytes 5898240 | tf_op jit(solution)/shard_map/reduce_scatter | solution.py:176
  13.0 118.0 %collective-permute-start = (bf16[8,20480]{1,0:T(8,128)(2,1)}, bf16[8,20480]{1,0:T(8,128)(2,1)}, u32[]{:S(2)}, u32[]{:S(2)}) collective-permute-start(bf16[8,20480]{1,0:T(8,128)(2,1)} %slice.53), channel_id=1, source_target_pairs={{0,8},{8,16},{16,24},{24,32},{32,40},{40,48},{48,56},{56,64},{64,7... | collective-permute-start | bytes 983048 | tf_op jit(solution)/shard_map/ppermute | solution.py:21
  91.5 1.4 copy-start.7
  106.6 1.5 copy-start.7
  120.0 4.6 %copy-start.9 = (pred[4,16]{1,0:T(4,128)(4,1)S(1)}, pred[4,16]{1,0:T(4,128)(4,1)}, u32[]{:S(2)}) copy-start(pred[4,16]{1,0:T(4,128)(4,1)} %and_reduce_fusion) | copy-start | bytes 196
  120.0 4.7 %copy-start.6 = (f32[1024,8]{0,1:T(8,128)S(1)}, f32[1024,8]{0,1:T(8,128)}, u32[]{:S(2)}) copy-start(f32[1024,8]{0,1:T(8,128)} %get-tuple-element.100) | copy-start | bytes 98308
  120.0 7.8 %copy-start.8 = (s32[4,256]{1,0:T(4,128)S(1)}, s32[4,256]{1,0:T(4,128)}, u32[]{:S(2)}) copy-start(s32[4,256]{1,0:T(4,128)} %add_add_fusion) | copy-start | bytes 12292
  134.5 12.5 %copy-start.2 = (bf16[4,256,8,192]{1,0,3,2:T(4,128)(2,1)S(1)}, bf16[4,256,8,192]{1,0,3,2:T(4,128)(2,1)}, u32[]{:S(2)}) copy-start(bf16[4,256,8,192]{1,0,3,2:T(4,128)(2,1)} %reshape.229) | copy-start | bytes 9437188
  221.6 4.5 %copy-start.3 = (f32[1024,8]{1,0:T(8,128)S(1)}, f32[1024,8]{1,0:T(8,128)}, u32[]{:S(2)}) copy-start(f32[1024,8]{1,0:T(8,128)} %copy.72) | copy-start | bytes 98308
  226.0 1.1 copy-start.4
  226.0 2.3 copy-start.5
  231.3 59.2 %copy-start.1 = (bf16[1024,768]{1,0:T(8,128)(2,1)S(1)}, bf16[1024,768]{1,0:T(8,128)(2,1)}, u32[]{:S(2)}) copy-start(bf16[1024,768]{1,0:T(8,128)(2,1)} %param.11) | copy-start | bytes 4718596
Sparse Core Ops, SparseCore 0:
  11.7 84.1 all-gather.1
  250.9 39.5 reduce-scatter.1
where the time goes:
time: 302 us; the launch traced here: 298 us
  matrix products  84.8 us (28%)
  local copies, waits for them, and re-layouts  74 us (25%)
  blocking collectives  49.2 us (16%)
  waiting for transfers between devices  39.7 us (13%)
  other arithmetic  30.4 us (10%)
  between operations  14.1 us (5%)
  starting transfers between devices  4.33 us (1%)
    reduce_scatter x1, waiting for transfers between devices, local(): lax.psum_scatter(jnp.dot(attended, out_weight, preferred_element_type=jnp...  39.7 us
    sub x2, matrix products, softmax_parts(): weights = jnp.where(keep_mask, jnp.exp(scores - row_top), 0.0)  36.3 us
    all_gather x1, blocking collectives, local(): lax.all_gather(comp_keys, 'ctx', axis=0, tiled=True)  26.6 us
    all_gather x1, blocking collectives, local(): lax.all_gather(comp_values, 'ctx', axis=0, tiled=True)  22.6 us
    dot_general x1, matrix products, local(): jnp.dot(attended, out_weight, preferred_element_type=jnp.float32)  19.5 us
    dot_general x1, matrix products, local(): jnp.einsum('uzai,uix->uzax', selected_weights, tiled_row_groups[..., QUER...  11.4 us
    sub x2, other arithmetic, softmax_parts(): weights = jnp.where(keep_mask, jnp.exp(scores - row_top), 0.0)  11.1 us
    gather x1, local copies, waits for them, and re-layouts, local(): tiled_row_groups = gathered[flat_picks]  9.79 us
  transfers between devices with their start and end apart: 3, of which 1 were waited for; matrix products, arithmetic and copies ran while one was open for 36% of the time, Pallas kernels for 0%

commit v1 on v0

--- a/solution.py
+++ b/solution.py
@@ -13,6 +13,15 @@
 WINDOW = 512
 QBLK = 256
 NEG_FILL = -1e30
+
+
+def end_group(point):
+    return jnp.concatenate(
+        lax.all_to_all(
+            jnp.stack(lax.axis_size("ctx") * [point]), axis_name="ctx", concat_axis=0, split_axis=0
+        ),
+        axis=0,
+    )
 
 
 def shifted(block, axis, distance):
@@ -67,7 +76,7 @@
         axis=1,
     ).astype(jnp.bfloat16)
     all_comp_keys, all_comp_values = (
-        lax.all_gather(comp_keys, "ctx", axis=0, tiled=True),
+        end_group(comp_keys),
         lax.all_gather(comp_values, "ctx", axis=0, tiled=True),
     )
     comp_count = all_comp_keys.shape[0]

time: 302 us -> 279 us (0.924)
  blocking collectives: 49.2 us -> 26.5 us
  other arithmetic: 30.4 us -> 22.8 us
  starting transfers between devices: 4.33 us -> 11.4 us
    all_gather x1 -> x0, blocking collectives: 26.6 us -> none  [local(): lax.all_gather(comp_keys, 'ctx', axis=0, tiled=True)]
    all_to_all x0 -> x1, starting transfers between devices: none -> 7.08 us  [end_group(): lax.all_to_all(jnp.stack(lax.axis_size('ctx') * [point]), axis_name='ctx'...]
    all_gather x1, blocking collectives: 22.6 us -> 26.5 us  [local(): lax.all_gather(comp_values, 'ctx', axis=0, tiled=True)]
    unnamed x23 -> x21, local copies, waits for them, and re-layouts: 7.02 us -> 7.06 us
  transfers between devices with their start and end apart: 3 -> 4, of which waited for: 1 -> 1; matrix products, arithmetic and copies ran while one was open for 36% -> 37% of each run, Pallas kernels for 0% -> 0%
where the time goes in v1:
time: 279 us; the launch traced here: 274 us
  matrix products  84.8 us (30%)
  local copies, waits for them, and re-layouts  73.7 us (26%)
  waiting for transfers between devices  39 us (14%)
  blocking collectives  26.5 us (9%)
  other arithmetic  22.8 us (8%)
  between operations  14.2 us (5%)
  starting transfers between devices  11.4 us (4%)
    reduce_scatter x1, waiting for transfers between devices, local(): lax.psum_scatter(jnp.dot(attended, out_weight, preferred_element_type=jnp...  39 us
    sub x2, matrix products, softmax_parts(): weights = jnp.where(keep_mask, jnp.exp(scores - row_top), 0.0)  36.4 us
    all_gather x1, blocking collectives, local(): lax.all_gather(comp_values, 'ctx', axis=0, tiled=True)  26.5 us
    dot_general x1, matrix products, local(): jnp.dot(attended, out_weight, preferred_element_type=jnp.float32)  19.5 us
    dot_general x1, matrix products, local(): jnp.einsum('uzai,uix->uzax', selected_weights, tiled_row_groups[..., QUER...  11.4 us
    sub x2, other arithmetic, softmax_parts(): weights = jnp.where(keep_mask, jnp.exp(scores - row_top), 0.0)  11.1 us
    gather x1, local copies, waits for them, and re-layouts, local(): tiled_row_groups = gathered[flat_picks]  9.79 us
    another operation x4, local copies, waits for them, and re-layouts, local(): jnp.stack([extended[span_index * QBLK:span_index * QBLK + WINDOW + QBLK]...  9.57 us
  transfers between devices with their start and end apart: 4, of which 1 were waited for; matrix products, arithmetic and copies ran while one was open for 37% of the time, Pallas kernels for 0%

profile of v1, /device:TPU:0, one launch (start us, length us, event | category | flops | bytes accessed | tf_op | source)
XLA Modules:
  0.0 273.7 jit_solution(13707045688515047286)
XLA Ops:
  13.0 4.3 %collective-permute-start = (bf16[8,20480]{1,0:T(8,128)(2,1)}, bf16[8,20480]{1,0:T(8,128)(2,1)}, u32[]{:S(2)}, u32[]{:S(2)}) collective-permute-start(bf16[8,20480]{1,0:T(8,128)(2,1)} %slice.53), channel_id=1, source_target_pairs={{0,8},{8,16},{16,24},{24,32},{32,40},{40,48},{48,56},{56,64},{64,7... | collective-permute-start | bytes 983048 | tf_op jit(solution)/shard_map/ppermute | solution.py:30
  19.3 7.1 %all-to-all-start = ((bf16[16,32,192]{2,1,0:T(8,128)(2,1)}), bf16[16,32,192]{2,1,0:T(8,128)(2,1)}, u32[]{:S(2)}, u32[]{:S(2)}) async-start(bf16[16,32,192]{2,1,0:T(8,128)(2,1)} %stack.12), calls=%async_computation | async-start | bytes 524288 | tf_op jit(solution)/shard_map/all_to_all | solution.py:20
  30.9 2.2 compare_and_fusion.1
  33.1 3.3 %compare_and_fusion = pred[4,256,1024]{1,2,0:T(8,128)(4,1)} fusion(s32[4,256]{1,0:T(4,128)S(1)} %add_add_fusion, s32[4,1024]{1,0:T(4,128)S(1)} %broadcast_add_fusion, pred[4,1024]{1,0:T(4,128)(4,1)S(1)} %and.51), kind=kLoop, calls=%fused_computation.55 | loop fusion | flops 2097152 | bytes 1073152 | tf_op jit(solution)/shard_map/and | solution.py:159
  36.4 3.2 %copy.50 = bf16[1024,1536]{0,1:T(8,128)(2,1)S(1)} copy(bf16[1024,1536]{1,0:T(8,128)(2,1)} %param.10) | data formatting | bytes 6291456 | tf_op args[0]
  39.7 4.0 %reshape.235 = bf16[4,256,8,192]{1,0,3,2:T(4,128)(2,1)} reshape(bf16[1024,1536]{0,1:T(8,128)(2,1)S(1)} %copy.50) | data formatting | bytes 6291456 | tf_op jit(solution)/shard_map/reshape | solution.py:61
  43.6 1.8 copy.49
  48.9 26.5 %all_gather.6 = bf16[512,128]{1,0:T(8,128)(2,1)} all-gather(bf16[32,128]{1,0:T(8,128)(2,1)S(1)} %multiply_reduce_fusion.1), channel_id=1, replica_groups=mesh['ctx'=16,'head'=8] {'ctx'}, dimensions={0}, use_global_device_ids=true | all-gather | bytes 139264 | tf_op jit(solution)/shard_map/all_gather | solution.py:80
  75.5 2.1 fusion.75
  78.6 28.9 %while.11 = (s32[]{:T(128)}, f32[2,512,8,128]{3,2,1,0:T(8,128)}, s32[2]{0:T(128)S(1)}, s32[1024]{0:T(1024)S(1)}, bf16[1024,8,192]{0,2,1:T(8,128)(2,1)S(1)}, /*in...) while((s32[]{:T(128)}, f32[2,512,8,128]{3,2,1,0:T(8,128)}, ...), condition=%wide.region_5.6_spmd.clone, body=%wide.region_2.5_spmd.clone.sunk | while | flops 1357649920 | bytes 34482888 | solution.py:103
  81.5 5.5 %fusion.113 = (f32[512,8]{0,1:T(8,128)S(1)}, bf16[512,8,512]{0,2,1:T(8,128)(2,1)}) fusion(f32[512,8,512]{0,2,1:T(8,128)S(1)} %fusion.112, pred[512,512]{0,1:T(8,128)(4,1)S(1)} %broadcast_compare_fusion.3), kind=kOutput, calls=%fused_computation.122.clone.1 | output fusion | flops 14680575 | bytes 12861440 | tf_op jit(solution)/shard_map/while/body/eval_jaxpr/sub | solution.py:35
  87.1 3.4 %divide_bitcast_fusion.2 = f32[1,512,8,128]{3,1,2,0:T(8,128)S(1)} fusion(bf16[512,8,512]{0,2,1:T(8,128)(2,1)} %get-tuple-element.158, f32[512,8]{0,1:T(8,128)S(1)} %broadcast_maximum_fusion.2, bf16[512,128]{1,0:T(8,128)(2,1)S(1)} %copy-done.7), kind=kOutput, calls=%fused_computation.13.clone.1 | convolution fusion | flops 537395200 | bytes 6438912 | tf_op jit(solution)/shard_map/while/body/eval_jaxpr/thn,nd->thd/dot_general | solution.py:98
  90.5 2.6 copy_dynamic-update-slice_fusion.2
  96.0 5.5 %fusion.113 = (f32[512,8]{0,1:T(8,128)S(1)}, bf16[512,8,512]{0,2,1:T(8,128)(2,1)}) fusion(f32[512,8,512]{0,2,1:T(8,128)S(1)} %fusion.112, pred[512,512]{0,1:T(8,128)(4,1)S(1)} %broadcast_compare_fusion.3), kind=kOutput, calls=%fused_computation.122.clone.1 | output fusion | flops 14680575 | bytes 12861440 | tf_op jit(solution)/shard_map/while/body/eval_jaxpr/sub | solution.py:35
  101.5 3.4 %divide_bitcast_fusion.2 = f32[1,512,8,128]{3,1,2,0:T(8,128)S(1)} fusion(bf16[512,8,512]{0,2,1:T(8,128)(2,1)} %get-tuple-element.158, f32[512,8]{0,1:T(8,128)S(1)} %broadcast_maximum_fusion.2, bf16[512,128]{1,0:T(8,128)(2,1)S(1)} %copy-done.7), kind=kOutput, calls=%fused_computation.13.clone.1 | convolution fusion | flops 537395200 | bytes 6438912 | tf_op jit(solution)/shard_map/while/body/eval_jaxpr/thn,nd->thd/dot_general | solution.py:98
  105.0 2.6 copy_dynamic-update-slice_fusion.2
  111.0 2.8 %stack.13 = bf16[1,768,320]{2,1,0:T(8,128)(2,1)} reshape(bf16[12,20480]{1,0:T(8,128)(2,1)} %get-tuple-element.96) | data formatting | bytes 983040 | tf_op jit(solution)/shard_map/stack | solution.py:108
  113.8 2.1 copy.66
  115.8 2.6 stack.14
  118.5 2.1 copy.67
  120.6 3.0 %pad_maximum_fusion = bf16[4,768,320]{1,2,0:T(8,128)(2,1)} fusion(bf16[1,768,320]{1,2,0:T(8,128)(2,1)} %get-tuple-element.99, bf16[1,768,320]{1,2,0:T(8,128)(2,1)} %get-tuple-element.98, bf16[1,768,320]{1,2,0:T(8,128)(2,1)} %copy.67, bf16[1,768,320]{1,2,0:T(8,128)(2,1)} %copy.66), kind=kLoop, calls=%fused_computation.68 | loop fusion | flops 2949120 | bytes 3932160 | tf_op jit(solution)/shard_map/stack | solution.py:108
  123.5 15.6 %fusion.88 = (f32[4,256,8]{1,2,0:T(8,128)S(1)}, bf16[4,256,8,768]{1,3,2,0:T(8,128)(2,1)}) fusion(pred[4,256,768]{1,2,0:T(8,128)(4,1)} %compare_and_fusion.1, bf16[4,256,8,192]{1,0,3,2:T(4,128)(2,1)S(1)} %copy-done.3, bf16[4,768,320]{1,2,0:T(8,128)(2,1)} %pad_maximum_fusion), kind=kOutput, calls=%fused_computation.124 | convolution fusion | flops 4875878912 | bytes 22839296 | tf_op jit(solution)/shard_map/sub | solution.py:35
  139.2 7.8 %broadcast_divide_fusion = f32[4,256,8,128]{3,1,2,0:T(8,128)S(1)} fusion(f32[4,256,8]{1,2,0:T(8,128)S(1)} %get-tuple-element.103, bf16[4,256,8,768]{1,3,2,0:T(8,128)(2,1)} %get-tuple-element.104, bf16[1,768,320]{1,2,0:T(8,128)(2,1)} %get-tuple-element.99, bf16[1,768,320]{1,2,0:T(8,128)(2,1)} %get-tuple-element.98, bf16[1,768,320]{1,2,0:T(8,128)(2,1)} %copy.67, ...), kind=kOutput, calls=%fused_computation.61 | convolution fusion | flops 1614807040 | bytes 18776064 | tf_op jit(solution)/shard_map/uzai,uix->uzax/dot_general | solution.py:136
  147.0 4.5 %copy.71 = f32[4,256,8,128]{3,2,1,0:T(8,128)} copy(f32[4,256,8,128]{3,1,2,0:T(8,128)S(1)} %broadcast_divide_fusion) | data formatting | bytes 8388608 | tf_op jit(solution)/shard_map/div | solution.py:136
  151.5 9.8 %gather_fusion = bf16[64,20480]{1,0:T(8,128)(2,1)S(1)} fusion(bf16[256,20480]{1,0:T(8,128)(2,1)} %all-gather.2.cloned.1.call-done, s32[1024]{0:T(1024)S(1)} %pad_clamp_fusion), kind=kCustom, calls=%fused_computation | custom fusion | bytes 5243136 | tf_op jit(solution)/shard_map/gather | solution.py:147
  161.3 4.7 %reshape.234 = bf16[4,1024,320]{2,1,0:T(8,128)(2,1)} reshape(bf16[64,20480]{1,0:T(8,128)(2,1)S(1)} %gather_fusion) | data formatting | bytes 5242880 | tf_op jit(solution)/shard_map/reshape | solution.py:148
  166.0 20.7 %fusion.93 = (f32[4,256,8]{1,2,0:T(8,128)S(1)}, bf16[4,256,8,1024]{1,3,2,0:T(8,128)(2,1)}) fusion(pred[4,256,1024]{1,2,0:T(8,128)(4,1)} %compare_and_fusion, bf16[4,256,8,192]{1,0,3,2:T(4,128)(2,1)} %reshape.235, bf16[4,1024,320]{2,1,0:T(8,128)(2,1)} %reshape.234), kind=kOutput, calls=%fused_computation.125 | convolution fusion | flops 6501172224 | bytes 29392896 | tf_op jit(solution)/shard_map/sub | solution.py:35
  186.7 11.4 %fusion.46 = f32[4,256,8,128]{3,1,2,0:T(8,128)S(1)} fusion(bf16[4,256,8,1024]{1,3,2,0:T(8,128)(2,1)} %get-tuple-element.106, f32[4,256,8]{1,2,0:T(8,128)S(1)} %get-tuple-element.105, bf16[4,1024,320]{2,1,0:T(8,128)(2,1)} %reshape.234), kind=kOutput, calls=%fused_computation.58 | convolution fusion | flops 2148532224 | bytes 22052864 | tf_op jit(solution)/shard_map/uzai,uix->uzax/dot_general | solution.py:171
  198.1 4.4 %copy.63 = f32[4,256,8,128]{3,2,1,0:T(8,128)} copy(f32[4,256,8,128]{3,1,2,0:T(8,128)S(1)} %fusion.46) | data formatting | bytes 8388608 | tf_op jit(solution)/shard_map/div | solution.py:171
  204.9 3.0 %mul.146 = f32[1024,8,128]{2,1,0:T(8,128)} broadcast(f32[1024,8]{1,0:T(8,128)S(1)} %copy-done.6), dimensions={0,1} | broadcast | bytes 4227072 | tf_op jit(solution)/shard_map/mul | solution.py:182
  207.9 19.5 %convolution_convert_fusion = bf16[1024,2560]{1,0:T(8,128)(2,1)} fusion(bf16[1024,2560]{1,0:T(8,128)(2,1)} %param.17, f32[128,8,8,128]{3,2,1,0:T(8,128)} %bitcast.148, f32[128,8,8,128]{3,2,1,0:T(8,128)} %bitcast.147, f32[128,8,8,128]{3,2,1,0:T(8,128)} %bitcast.149, f32[128,8,8,128]{3,2,1,0:T(8,128)S(1)} %bitcast.146, f32[128,8,8,128]{3,2,1,0:T(8,128)} %bitcast.33, ...), kind=kOutput, calls=%fused_computation.48 | convolution fusion | flops 5377622016 | bytes 35651584 | tf_op jit(solution)/shard_map/dot_general | solution.py:186
  227.4 39.0 %reduce-scatter.2.cloned.1.call-done = bf16[128,2560]{1,0:T(8,128)(2,1)} async-done(((bf16[1024,2560]{1,0:T(8,128)(2,1)}), bf16[128,2560]{1,0:T(8,128)(2,1)}) %reduce-scatter.2.cloned.1.call-update) | async-done | bytes 655376 | tf_op jit(solution)/shard_map/reduce_scatter | solution.py:185
  (90 shorter events, 27.8 us)
Async XLA Ops:
  6.5 1.4 copy-start
  6.5 145.0 %all-gather.2.cloned.1.call-start = ((), (), s32[]{:S(2)}) async-start(), calls=%async_computation.2 | async-start | bytes 11141120 | tf_op jit(solution)/shard_map/all_gather | solution.py:146
  9.5 26.9 %copy-start.2 = (bf16[1024,128]{0,1:T(8,128)(2,1)}, bf16[1024,128]{0,1:T(8,128)(2,1)S(1)}, u32[]{:S(2)}) copy-start(bf16[1024,128]{0,1:T(8,128)(2,1)S(1)} %copy.84) | copy-start | bytes 786436
  11.6 18.6 %copy-start.8 = (f32[1024,3,8]{0,2,1:T(8,128)S(1)}, f32[1024,3,8]{0,2,1:T(8,128)}, u32[]{:S(2)}) copy-start(f32[1024,3,8]{0,2,1:T(8,128)} %param.16) | copy-start | bytes 294916
  13.0 94.6 %collective-permute-start = (bf16[8,20480]{1,0:T(8,128)(2,1)}, bf16[8,20480]{1,0:T(8,128)(2,1)}, u32[]{:S(2)}, u32[]{:S(2)}) collective-permute-start(bf16[8,20480]{1,0:T(8,128)(2,1)} %slice.53), channel_id=1, source_target_pairs={{0,8},{8,16},{16,24},{24,32},{32,40},{40,48},{48,56},{56,64},{64,7... | collective-permute-start | bytes 983048 | tf_op jit(solution)/shard_map/ppermute | solution.py:30
  19.3 58.2 %all-to-all-start = ((bf16[16,32,192]{2,1,0:T(8,128)(2,1)}), bf16[16,32,192]{2,1,0:T(8,128)(2,1)}, u32[]{:S(2)}, u32[]{:S(2)}) async-start(bf16[16,32,192]{2,1,0:T(8,128)(2,1)} %stack.12), calls=%async_computation | async-start | bytes 524288 | tf_op jit(solution)/shard_map/all_to_all | solution.py:20
  26.4 240.0 %reduce-scatter.2.cloned.1.call-start = ((), (), s32[]{:S(2)}) async-start(), calls=%async_computation.3 | async-start | bytes 5898240 | tf_op jit(solution)/shard_map/reduce_scatter | solution.py:185
  81.5 5.5 %copy-start.7 = (bf16[512,128]{1,0:T(8,128)(2,1)S(1)}, bf16[512,128]{1,0:T(8,128)(2,1)}, u32[]{:S(2)}) copy-start(bf16[512,128]{1,0:T(8,128)(2,1)} %get-tuple-element.188) | copy-start | bytes 393220 | tf_op jit(solution)/shard_map/while
  96.0 5.5 %copy-start.7 = (bf16[512,128]{1,0:T(8,128)(2,1)S(1)}, bf16[512,128]{1,0:T(8,128)(2,1)}, u32[]{:S(2)}) copy-start(bf16[512,128]{1,0:T(8,128)(2,1)} %get-tuple-element.188) | copy-start | bytes 393220 | tf_op jit(solution)/shard_map/while
  111.0 12.5 %copy-start.3 = (bf16[4,256,8,192]{1,0,3,2:T(4,128)(2,1)S(1)}, bf16[4,256,8,192]{1,0,3,2:T(4,128)(2,1)}, u32[]{:S(2)}) copy-start(bf16[4,256,8,192]{1,0,3,2:T(4,128)(2,1)} %reshape.235) | copy-start | bytes 9437188
  198.1 4.5 %copy-start.4 = (f32[1024,8]{1,0:T(8,128)S(1)}, f32[1024,8]{1,0:T(8,128)}, u32[]{:S(2)}) copy-start(f32[1024,8]{1,0:T(8,128)} %copy.49) | copy-start | bytes 98308
  202.6 1.1 copy-start.5
  202.6 2.3 copy-start.6
  207.9 58.5 %copy-start.1 = (bf16[1024,768]{1,0:T(8,128)(2,1)S(1)}, bf16[1024,768]{1,0:T(8,128)(2,1)}, u32[]{:S(2)}) copy-start(bf16[1024,768]{1,0:T(8,128)(2,1)} %param.11) | copy-start | bytes 4718596
Sparse Core Ops, SparseCore 0:
  11.7 86.4 all-gather.1
  227.5 38.8 reduce-scatter.1
